TPU v7x, 1024 devices: a whole 4x4x32 slice. The times are simulated.
1024 devices in a mesh: slab: 32 (over x, y, core), group: 32 (over z).
Axes of the slice: x: 4, y: 4, z: 32, core: 2. Of those that a mesh axis runs over, the one named last changes fastest.
Arguments:
- grads: bfloat16 [256, 2048, 512], P('group', 'slab'), may hold values from -64 to 64
- grad_slot: int32 [32, 8], P('group'), may hold values from 0 to 7, each once within a row
- momentum: bfloat16 [256, 2048, 512], P('group', 'slab'), may hold values from -6 to 6
Outputs:
- new_momentum: bfloat16 [256, 2048, 512], P('group', 'slab')
- update: bfloat16 [256, 2048, 512], P('group', 'slab')
All inputs are finite; a program needn't handle non-finite values.
Results may differ from a plain program's by a relative error of at most 0.0071.
Values may be sent and summed in bfloat16 or wider, within the bound.
A program may use at most 32 MiB of HBM per device.

v0:
```python
import jax
import jax.numpy as jnp
from jax import lax
from jax.sharding import PartitionSpec as P

M = 2048
SHARE = 4
ITERS = 2


COEF_A = 3.4445
COEF_B = -4.775
COEF_C = 2.0315
DECAY_RATE = 0.95


def form_gram(matrix):
    return lax.dot_general(
        matrix, matrix, (((0,), (0,)), ((), ())), preferred_element_type=jnp.float32
    )


def newton_factor(current):
    identity = jnp.eye(current.shape[0], dtype=jnp.float32)
    product = current
    for iteration in range(ITERS):
        rounded = current.astype(jnp.bfloat16)
        squared = jnp.dot(rounded, rounded, preferred_element_type=jnp.float32)
        poly = COEF_A * identity + COEF_B * current + COEF_C * squared
        poly_half = poly.astype(jnp.bfloat16)
        if iteration == 0:
            product = poly
        else:
            product = jnp.dot(
                product.astype(jnp.bfloat16), poly_half, preferred_element_type=jnp.float32
            )
        if iteration < ITERS - 1:
            halfway = jnp.dot(rounded, poly_half, preferred_element_type=jnp.float32).astype(
                jnp.bfloat16
            )
            current = jnp.dot(poly_half, halfway, preferred_element_type=jnp.float32)
    return product


def on_device(grads, grad_slot, momentum):
    partial_sq = jnp.sum(jnp.square(grads.astype(jnp.float32)))
    total_sq = lax.psum(partial_sq, ("slab", "group"))
    entries = grads.size * lax.axis_size("slab") * lax.axis_size("group")
    root_mean = jnp.sqrt(total_sq / entries + 1e-06)
    clip_factor = jnp.minimum(1.0, 1.0 / root_mean)
    ordered = jnp.take(grads, grad_slot[0], axis=0)
    new_momentum = (
        DECAY_RATE * momentum.astype(jnp.float32) + clip_factor * ordered.astype(jnp.float32)
    ).astype(jnp.bfloat16)
    experts, slab_rows, columns = new_momentum.shape
    slab_count = lax.axis_size("slab")
    quarter = slab_rows // SHARE
    outgoing = jnp.repeat(new_momentum, SHARE, axis=0)
    whole_matrix = lax.all_to_all(outgoing, "slab", split_axis=0, concat_axis=1, tiled=True)[0]
    gram_matrix = form_gram(whole_matrix)
    offset = lax.axis_index("slab") % SHARE * quarter
    own_rows = lax.dynamic_slice_in_dim(
        whole_matrix.reshape(slab_count, slab_rows, columns), offset, quarter, 1
    )
    frobenius = jnp.trace(gram_matrix) + 1e-06
    product = newton_factor(gram_matrix / frobenius)
    scaled_q = (product / jnp.sqrt(frobenius)).astype(jnp.bfloat16)
    result_rows = jnp.dot(
        own_rows.reshape(slab_count * quarter, columns),
        scaled_q,
        preferred_element_type=jnp.float32,
    )
    scaled_rows = (
        (jnp.sqrt(jnp.float32(M)) * result_rows)
        .astype(jnp.bfloat16)
        .reshape(slab_count, quarter, columns)
    )
    returned = lax.all_to_all(scaled_rows, "slab", split_axis=0, concat_axis=0, tiled=True)
    update = returned.reshape(experts, SHARE, quarter, columns).reshape(experts, slab_rows, columns)
    return (new_momentum, update)


def solution(mesh):
    in_specs = (P("group", "slab", None), P("group", None), P("group", "slab", None))
    out_specs = (P("group", "slab", None), P("group", "slab", None))
    return jax.shard_map(
        on_device, mesh=mesh, in_specs=in_specs, out_specs=out_specs, check_vma=False
    )
```

profile of v0, /device:TPU:1, one launch (start us, length us, event | category | flops | bytes accessed | tf_op | source)
XLA Modules:
  0.0 238.2 jit_solution(13240306373614766624)
XLA Ops:
  0.6 0.7 fusion.13
  1.3 0.7 compare_and_fusion
  2.0 1.9 multiply_reduce_fusion
  3.9 1.6 gather_fusion
  5.5 170.4 %psum.7 = f32[]{:T(128)} all-reduce(f32[]{:T(128)} %multiply_reduce_fusion), channel_id=1, replica_groups=mesh['slab'=32,'group'=32] {'slab','group'}, use_global_device_ids=true, to_apply=%region_1.0 | all-reduce | flops 1 | bytes 8 | tf_op jit(solution)/shard_map/psum | solution.py:47
  176.6 1.3 add_convert_fusion
  177.9 0.0 copy-start
  177.9 1.6 broadcast_in_dim.17
  179.5 0.0 copy-done
  179.5 4.5 %all-to-all-start = ((bf16[32,64,512]{2,1,0:T(8,128)(2,1)}), bf16[32,64,512]{2,1,0:T(8,128)(2,1)S(1)}, u32[]{:S(2)}, u32[]{:S(2)}) async-start(bf16[32,64,512]{2,1,0:T(8,128)(2,1)} %bitcast.3), calls=%async_computation | async-start | bytes 4194304 | tf_op jit(solution)/shard_map/all_to_all | solution.py:59
  184.0 28.4 %all-to-all-done = bf16[32,64,512]{2,1,0:T(8,128)(2,1)S(1)} async-done(((bf16[32,64,512]{2,1,0:T(8,128)(2,1)}), bf16[32,64,512]{2,1,0:T(8,128)(2,1)S(1)}, u32[]{:S(2)}, u32[]{:S(2)}) %all-to-all-start) | async-done | bytes 2097184 | tf_op jit(solution)/shard_map/all_to_all | solution.py:59
  212.4 1.9 select_reduce_fusion
  214.3 0.0 copy-start.1
  215.0 0.3 copy-done.1
  215.3 1.3 fusion.2
  216.6 2.3 fusion.6
  218.9 1.3 fusion.3
  220.2 2.0 fusion.5
  222.2 15.2 %all_to_all.14 = bf16[32,16,512]{2,1,0:T(8,128)(2,1)S(1)} all-to-all(bf16[32,16,512]{2,1,0:T(8,128)(2,1)S(1)} %bitcast.20), channel_id=1, replica_groups=mesh['slab'=32,'group'=32] {'slab'}, dimensions={0} | all-to-all | bytes 1048576 | tf_op jit(solution)/shard_map/all_to_all | solution.py:78
  237.4 0.8 copy.6
  (2 shorter events, 0.0 us)
Async XLA Ops:
  177.9 1.6 copy-start
  179.5 32.9 %all-to-all-start = ((bf16[32,64,512]{2,1,0:T(8,128)(2,1)}), bf16[32,64,512]{2,1,0:T(8,128)(2,1)S(1)}, u32[]{:S(2)}, u32[]{:S(2)}) async-start(bf16[32,64,512]{2,1,0:T(8,128)(2,1)} %bitcast.3), calls=%async_computation | async-start | bytes 4194304 | tf_op jit(solution)/shard_map/all_to_all | solution.py:59
  214.3 1.0 copy-start.1
where the time goes:
time: 239 us; the launch traced here: 238 us
  blocking collectives  186 us (78%)
  waiting for transfers between devices  28.4 us (12%)
  matrix products  8.69 us (4%)
  other arithmetic  4.56 us (2%)
  starting transfers between devices  4.49 us (2%)
  local copies, waits for them, and re-layouts  4.35 us (2%)
    psum x1, blocking collectives, on_device(): total_sq = lax.psum(partial_sq, ('slab', 'group'))  170 us
    all_to_all x1, waiting for transfers between devices, on_device(): lax.all_to_all(outgoing, 'slab', split_axis=0, concat_axis=1, tiled=True)[0]  28.4 us
    all_to_all x1, blocking collectives, on_device(): lax.all_to_all(scaled_rows, 'slab', split_axis=0, concat_axis=0, tiled=True)  15.2 us
  transfers between devices with their start and end apart: 1, of which 1 were waited for; matrix products, arithmetic and copies ran while one was open for 0% of the time, Pallas kernels for 0%

commit v1 on v0

v1 whole, which is shorter than its diff:
```python
import jax
import jax.numpy as jnp
from jax import lax
from jax.experimental import pallas as pl
from jax.experimental.pallas import tpu as pltpu
from jax.sharding import PartitionSpec as P

MESH = pl.DeviceIdType.MESH

SIDE = 4
CORES = 2
SLABS = SIDE * SIDE * CORES
CHIPS = SIDE * SIDE
GROUPS = 32
EXPERTS = 8
ROWS = 64
M = SLABS * ROWS
K = 512
HALF = K // 2
OWN = CHIPS * ROWS
REACH = 4

COEF_A = 3.4445
COEF_B = -4.775
COEF_C = 2.0315
DECAY_RATE = 0.95
ENTRIES = GROUPS * EXPERTS * M * K

COLUMNS = (2, 1, 3, 0)
NEAR = tuple(off for off in range(-REACH, REACH) if off != 0)


def squares(block):
    wide = block.astype(jnp.float32)
    return jnp.sum((wide * wide).reshape(ROWS // 8, 8, K), axis=0)


def fresh(moment, gradient, factor):
    return (
        DECAY_RATE * moment.astype(jnp.float32) + factor * gradient.astype(jnp.float32)
    ).astype(jnp.bfloat16)


def dot(left, right):
    return jnp.dot(left, right, preferred_element_type=jnp.float32)


def kernel(
    slot_ref,
    grads_hbm,
    momentum_hbm,
    new_ref,
    update_ref,
    grads_in,
    pair,
    raw,
    own_new,
    part,
    slab_parts,
    plane,
    near_parts,
    window,
    window_parts,
    wide_window,
    wide_parts,
    far_parts,
    gram_own,
    gram_other,
    current,
    rounded,
    poly_first,
    halfway,
    poly_second,
    scaled,
    outgoing,
    load_sem,
    slab_send,
    slab_recv,
    near_send,
    near_recv,
    step_send,
    step_recv,
    raw_send,
    raw_recv,
    local_sem,
    gram_send,
    gram_recv,
    back_send,
    back_recv,
):
    slab = lax.axis_index("slab")
    group = lax.axis_index("group")
    chip = slab // CORES
    core = slab % CORES
    x = chip // SIDE
    y = chip % SIDE
    active = (x + y) % 2 == 0
    mine = x * 2 + y // 2

    def along_slab(other):
        return (other, group)

    def along_group(offset):
        return (slab, (group + offset + GROUPS) % GROUPS)

    def send(src, dst, send_sem, recv_sem, device):
        return pltpu.make_async_remote_copy(
            src_ref=src,
            dst_ref=dst,
            send_sem=send_sem,
            recv_sem=recv_sem,
            device_id=device,
            device_id_type=MESH,
        )

    load_grads = pltpu.make_async_copy(grads_hbm, grads_in, load_sem.at[0])
    load_momentum = pltpu.make_async_copy(momentum_hbm, pair.at[0], load_sem.at[1])
    load_grads.start()
    load_momentum.start()

    barrier = pltpu.get_barrier_semaphore()
    for offset in NEAR + (REACH,):
        pl.semaphore_signal(barrier, inc=1, device_id=along_group(offset), device_id_type=MESH)

    @pl.loop(1, SLABS)
    def _(step):
        pl.semaphore_signal(
            barrier, inc=1, device_id=along_slab((slab + step) % SLABS), device_id_type=MESH
        )

    load_grads.wait()
    total = jnp.zeros((8, K), jnp.float32)
    for expert in range(EXPERTS):
        block = grads_in[slot_ref[0, expert]]
        pair[1, expert] = block
        total += squares(block)
    lanes = total[:, :128] + total[:, 128:256] + total[:, 256:384] + total[:, 384:]
    part[...] = jnp.sum(lanes, axis=0, keepdims=True)
    load_momentum.wait()
    pl.semaphore_wait(barrier, SLABS - 1 + len(NEAR) + 1)

    def slab_copy(step):
        return send(
            part,
            slab_parts.at[step],
            slab_send.at[step],
            slab_recv.at[step],
            along_slab((slab + step) % SLABS),
        )

    @pl.loop(1, SLABS)
    def _(step):
        slab_copy(step).start()

    def raw_copies(hops, which):
        column = (x + hops) % SIDE
        expert = column * 2 + which
        row = which * 2 + column % 2
        place = ((x + SIDE - column) % SIDE) * SIDE + (y + SIDE - row) % SIDE
        target = (column * SIDE + row) * CORES + core
        index = COLUMNS.index(hops) * 2 + which
        return target, expert, [
            send(
                pair.at[kind, expert],
                raw.at[kind, place],
                raw_send.at[kind, index],
                raw_recv.at[kind, place],
                along_slab(target),
            )
            for kind in range(2)
        ]

    def local_copies(expert):
        return [
            pltpu.make_async_copy(pair.at[kind, expert], raw.at[kind, 0], local_sem.at[kind])
            for kind in range(2)
        ]

    for hops in COLUMNS:
        for which in range(2):
            target, expert, copies = raw_copies(hops, which)

            @pl.when(target != slab)
            def _():
                for copy in copies:
                    copy.start()

    @pl.when(active)
    def _():
        for copy in local_copies(mine):
            copy.start()

    @pl.loop(1, SLABS)
    def _(step):
        slab_copy(step).wait_recv()

    plane[...] = part[...] + jnp.sum(slab_parts[1:], axis=0)

    near_copies = [
        send(
            plane,
            near_parts.at[index],
            near_send.at[index],
            near_recv.at[index],
            along_group(offset),
        )
        for index, offset in enumerate(NEAR)
    ]

    def step_copies(src, dst, stage):
        return [
            send(
                src(side),
                dst.at[side],
                step_send.at[stage, side],
                step_recv.at[stage, side],
                along_group(offset),
            )
            for side, offset in enumerate((REACH, -REACH))
        ]

    window_copies = step_copies(lambda side: window, window_parts, 0)
    wide_copies = step_copies(lambda side: wide_window, wide_parts, 1)
    far_copies = step_copies(lambda side: wide_parts.at[side], far_parts, 2)

    for copy in near_copies:
        copy.start()
    for copy in near_copies:
        copy.wait_recv()
    window[...] = plane[...] + jnp.sum(near_parts[...], axis=0)
    for copy in window_copies:
        copy.start()
    for copy in window_copies:
        copy.wait_recv()
    wide_window[...] = jnp.sum(window_parts[...], axis=0)
    for copy in wide_copies:
        copy.start()
    for copy, forward in zip(wide_copies, far_copies):
        copy.wait_recv()
        forward.start()
    for copy in far_copies:
        copy.wait_recv()

    total_sq = jnp.sum(jnp.sum(far_parts[...], axis=0), axis=1, keepdims=True)
    root_mean = jnp.sqrt(total_sq / ENTRIES + 1e-06)
    factor = jnp.minimum(1.0, 1.0 / root_mean)

    def own_result():
        for expert in range(EXPERTS):
            new_ref[expert] = fresh(pair[0, expert], pair[1, expert], factor)

    def gram_copies():
        partner = along_slab(chip * CORES + 1 - core)
        return [
            send(
                gram_own.at[index],
                gram_other.at[index],
                gram_send.at[index],
                gram_recv.at[index],
                partner,
            )
            for index in range(3)
        ]

    def back_copy(hops_x, hops_y):
        place = hops_x * SIDE + hops_y
        target = ((x + hops_x) % SIDE * SIDE + (y + hops_y) % SIDE) * CORES + core
        return send(
            outgoing.at[place],
            update_ref.at[mine],
            back_send.at[place],
            back_recv.at[mine],
            along_slab(target),
        )

    @pl.when(active)
    def _():
        for copy in local_copies(mine):
            copy.wait()

        @pl.loop(1, CHIPS)
        def _(place):
            for kind in range(2):
                send(
                    pair.at[kind, 0],
                    raw.at[kind, place],
                    raw_send.at[kind, 0],
                    raw_recv.at[kind, place],
                    along_slab(slab),
                ).wait_recv()

        for place in range(CHIPS):
            own_new[place * ROWS : (place + 1) * ROWS, :] = fresh(
                raw[0, place], raw[1, place], factor
            )

        for index, (left, right) in enumerate(((0, 0), (0, 1), (1, 1))):
            gram_own[index] = lax.dot_general(
                own_new[:, left * HALF : (left + 1) * HALF],
                own_new[:, right * HALF : (right + 1) * HALF],
                (((0,), (0,)), ((), ())),
                preferred_element_type=jnp.float32,
            )
            if index > 0:
                gram_copies()[index - 1].start()
        gram_copies()[2].start()
        for copy in gram_copies():
            copy.wait_recv()

        trace = jnp.zeros((128, 128), jnp.float32)
        for index in (0, 2):
            whole = gram_own[index] + gram_other[index]
            gram_own_low, gram_own_high = whole[:128, :128], whole[128:, 128:]
            trace += gram_own_low + gram_own_high
        eye = lax.broadcasted_iota(jnp.int32, (128, 128), 0) == lax.broadcasted_iota(
            jnp.int32, (128, 128), 1
        )
        trace = jnp.where(eye, trace, 0.0)
        frobenius = (
            jnp.sum(jnp.sum(trace, axis=0, keepdims=True), axis=1, keepdims=True) + 1e-06
        )
        inverse = 1.0 / frobenius
        for index, (left, right) in enumerate(((0, 0), (0, 1), (1, 1))):
            block = (gram_own[index] + gram_other[index]) * inverse
            current[left * HALF : (left + 1) * HALF, right * HALF : (right + 1) * HALF] = block
            rounded[left * HALF : (left + 1) * HALF, right * HALF : (right + 1) * HALF] = (
                block.astype(jnp.bfloat16)
            )
            if index == 1:
                block = block.T
                current[HALF:, :HALF] = block
                rounded[HALF:, :HALF] = block.astype(jnp.bfloat16)

        def polynomial(into, start):
            rows = slice(start, start + HALF)
            squared = dot(rounded[rows, :], rounded[...])
            diagonal = lax.broadcasted_iota(jnp.int32, (HALF, K), 0) + start
            identity = jnp.where(
                diagonal == lax.broadcasted_iota(jnp.int32, (HALF, K), 1), COEF_A, 0.0
            )
            into[rows, :] = (identity + COEF_B * current[rows, :] + COEF_C * squared).astype(
                jnp.bfloat16
            )

        halves = (0, HALF)
        for start in halves:
            polynomial(poly_first, start)
        for start in halves:
            rows = slice(start, start + HALF)
            halfway[rows, :] = dot(rounded[rows, :], poly_first[...]).astype(jnp.bfloat16)
        for start in halves:
            rows = slice(start, start + HALF)
            following = dot(poly_first[rows, :], halfway[...])
            current[rows, :] = following
            rounded[rows, :] = following.astype(jnp.bfloat16)
        for start in halves:
            polynomial(poly_second, start)
        root = 1.0 / jnp.sqrt(frobenius)
        for start in halves:
            rows = slice(start, start + HALF)
            scaled[rows, :] = (dot(poly_first[rows, :], poly_second[...]) * root).astype(
                jnp.bfloat16
            )

        for turn, hops_x in enumerate(COLUMNS):
            start = hops_x * SIDE * ROWS
            result = jnp.sqrt(jnp.float32(M)) * dot(
                own_new[start : start + SIDE * ROWS, :], scaled[...]
            )
            outgoing[hops_x * SIDE : (hops_x + 1) * SIDE] = result.astype(jnp.bfloat16).reshape(
                SIDE, ROWS, K
            )
            if turn > 0:
                for hops_y in COLUMNS:
                    back_copy(COLUMNS[turn - 1], hops_y).start()
        for hops_y in COLUMNS[:-1]:
            back_copy(0, hops_y).start()
        update_ref[mine] = outgoing[0]

    own_result()

    for hops in COLUMNS:
        for which in range(2):
            target, expert, copies = raw_copies(hops, which)

            @pl.when(target != slab)
            def _():
                for copy in copies:
                    copy.wait_send()
                send(
                    outgoing.at[0],
                    update_ref.at[expert],
                    back_send.at[0],
                    back_recv.at[expert],
                    along_slab(target),
                ).wait_recv()

    @pl.when(active)
    def _():
        for copy in gram_copies():
            copy.wait_send()
        for hops_x in COLUMNS:
            for hops_y in COLUMNS:
                if (hops_x, hops_y) != (0, 0):
                    back_copy(hops_x, hops_y).wait_send()

    @pl.loop(1, SLABS)
    def _(step):
        slab_copy(step).wait_send()

    for copy in near_copies + window_copies + wide_copies + far_copies:
        copy.wait_send()


def on_device(grads, grad_slot, momentum):
    shape = jax.ShapeDtypeStruct(grads.shape, jnp.bfloat16)
    scalar = (1, 128)
    dma = pltpu.SemaphoreType.DMA
    return pl.pallas_call(
        kernel,
        out_shape=(shape, shape),
        in_specs=[
            pl.BlockSpec(memory_space=pltpu.SMEM),
            pl.BlockSpec(memory_space=pl.ANY),
            pl.BlockSpec(memory_space=pl.ANY),
        ],
        out_specs=(pl.BlockSpec(memory_space=pltpu.VMEM),) * 2,
        scratch_shapes=[
            pltpu.VMEM((EXPERTS, ROWS, K), jnp.bfloat16),
            pltpu.VMEM((2, EXPERTS, ROWS, K), jnp.bfloat16),
            pltpu.VMEM((2, CHIPS, ROWS, K), jnp.bfloat16),
            pltpu.VMEM((OWN, K), jnp.bfloat16),
            pltpu.VMEM(scalar, jnp.float32),
            pltpu.VMEM((SLABS, *scalar), jnp.float32),
            pltpu.VMEM(scalar, jnp.float32),
            pltpu.VMEM((len(NEAR), *scalar), jnp.float32),
            pltpu.VMEM(scalar, jnp.float32),
            pltpu.VMEM((2, *scalar), jnp.float32),
            pltpu.VMEM(scalar, jnp.float32),
            pltpu.VMEM((2, *scalar), jnp.float32),
            pltpu.VMEM((2, *scalar), jnp.float32),
            pltpu.VMEM((3, HALF, HALF), jnp.float32),
            pltpu.VMEM((3, HALF, HALF), jnp.float32),
            pltpu.VMEM((K, K), jnp.float32),
            pltpu.VMEM((K, K), jnp.bfloat16),
            pltpu.VMEM((K, K), jnp.bfloat16),
            pltpu.VMEM((K, K), jnp.bfloat16),
            pltpu.VMEM((K, K), jnp.bfloat16),
            pltpu.VMEM((K, K), jnp.bfloat16),
            pltpu.VMEM((CHIPS, ROWS, K), jnp.bfloat16),
            dma((2,)),
            dma((SLABS,)),
            dma((SLABS,)),
            dma((len(NEAR),)),
            dma((len(NEAR),)),
            dma((3, 2)),
            dma((3, 2)),
            dma((2, EXPERTS)),
            dma((2, CHIPS)),
            dma((2,)),
            dma((3,)),
            dma((3,)),
            dma((CHIPS,)),
            dma((EXPERTS,)),
        ],
        compiler_params=pltpu.CompilerParams(collective_id=0, has_side_effects=True),
        name="muon_step",
    )(grad_slot, grads, momentum)


def solution(mesh):
    in_specs = (P("group", "slab", None), P("group", None), P("group", "slab", None))
    out_specs = (P("group", "slab", None), P("group", "slab", None))
    return jax.shard_map(
        on_device, mesh=mesh, in_specs=in_specs, out_specs=out_specs, check_vma=False
    )
```

time: 239 us -> 87.9 us (0.37)
  blocking collectives: 186 us -> 0 us
  Pallas kernels: 0 us -> 84.3 us
  waiting for transfers between devices: 28.4 us -> 0 us
  matrix products: 8.69 us -> 0 us
  other arithmetic: 4.56 us -> 0 us
  starting transfers between devices: 4.49 us -> 0 us
    psum x1 -> x0, blocking collectives: 170 us -> none  [on_device(): total_sq = lax.psum(partial_sq, ('slab', 'group'))]
    pallas_call x0 -> x1, Pallas kernels: none -> 84.3 us  [on_device(): pl.pallas_call(kernel, out_shape=(shape, shape), in_specs=[pl.BlockSpec(m...]
    all_to_all x1 -> x0, waiting for transfers between devices: 28.4 us -> none  [on_device(): lax.all_to_all(outgoing, 'slab', split_axis=0, concat_axis=1, tiled=True)[0]]
    all_to_all x1 -> x0, blocking collectives: 15.2 us -> none  [on_device(): lax.all_to_all(scaled_rows, 'slab', split_axis=0, concat_axis=0, tiled=True)]
    dot_general x5 -> x0, matrix products: 8.69 us -> none  [the longest x2 2.54 us: newton_factor(): squared = jnp.dot(rounded, rounded, preferred_element_type=jnp.float32)]
    all_to_all x1 -> x0, starting transfers between devices: 4.49 us -> none  [on_device(): lax.all_to_all(outgoing, 'slab', split_axis=0, concat_axis=1, tiled=True)[0]]
  transfers between devices with their start and end apart: 1 -> 0, of which waited for: 1 -> 0; matrix products, arithmetic and copies ran while one was open for 0% -> 0% of each run, Pallas kernels for 0% -> 0%
where the time goes in v1:
time: 87.9 us; the launch traced here: 87.7 us
  Pallas kernels  84.3 us (96%)
  local copies, waits for them, and re-layouts  2.72 us (3%)
    pallas_call x1, Pallas kernels, on_device(): pl.pallas_call(kernel, out_shape=(shape, shape), in_specs=[pl.BlockSpec(m...  84.3 us
    unnamed x4, local copies, waits for them, and re-layouts  2.72 us

profile of v1, /device:TPU:1, one launch (start us, length us, event | category | flops | bytes accessed | tf_op | source)
XLA Modules:
  0.0 87.7 jit_solution(2200897525453615975)
XLA Ops:
  0.6 84.3 %muon_step.1 = (bf16[8,64,512]{2,1,0:T(8,128)(2,1)}, bf16[8,64,512]{2,1,0:T(8,128)(2,1)}) custom-call(s32[1,8]{1,0:T(1,128)} %slot_ref.1, bf16[8,64,512]{2,1,0:T(8,128)(2,1)} %grads_hbm.1, bf16[8,64,512]{2,1,0:T(8,128)(2,1)} %momentum_hbm.1), custom_call_target="tpu_custom_call" | custom-call | tf_op jit(solution)/shard_map/muon_step/pallas_call | solution.py:419
  85.0 0.0 copy-start
  85.0 1.9 %copy.7 = bf16[8,64,512]{2,1,0:T(8,128)(2,1)} copy(bf16[8,64,512]{2,1,0:T(8,128)(2,1)} %get-tuple-element.4) | data formatting | bytes 1048576
  86.9 0.0 copy-done
  86.9 0.8 copy.8
Async XLA Ops:
  85.0 1.9 %copy-start = (bf16[8,64,512]{2,1,0:T(8,128)(2,1)S(1)}, bf16[8,64,512]{2,1,0:T(8,128)(2,1)}, u32[]{:S(2)}) copy-start(bf16[8,64,512]{2,1,0:T(8,128)(2,1)} %get-tuple-element.5) | copy-start | bytes 1572868

commit v2 on v1

--- a/solution.py
+++ b/solution.py
@@ -27,6 +27,7 @@
 ENTRIES = GROUPS * EXPERTS * M * K
 
 COLUMNS = (2, 1, 3, 0)
+BACK_RELAYED = ((2, 1), (2, 3), (1, 1), (3, 3))
 NEAR = tuple(off for off in range(-REACH, REACH) if off != 0)
 
 
@@ -46,14 +47,17 @@
 
 
 def kernel(
-    slot_ref,
+    slot_hbm,
     grads_hbm,
     momentum_hbm,
     new_ref,
     update_ref,
+    slot_ref,
     grads_in,
     pair,
     raw,
+    relayed,
+    back_relayed,
     own_new,
     part,
     slab_parts,
@@ -62,7 +66,6 @@
     window,
     window_parts,
     wide_window,
-    wide_parts,
     far_parts,
     gram_own,
     gram_other,
@@ -82,11 +85,15 @@
     step_recv,
     raw_send,
     raw_recv,
+    relay_send,
+    relay_recv,
     local_sem,
     gram_send,
     gram_recv,
     back_send,
     back_recv,
+    back_relay_send,
+    back_relay_recv,
 ):
     slab = lax.axis_index("slab")
     group = lax.axis_index("group")
@@ -100,6 +107,9 @@
     def along_slab(other):
         return (other, group)
 
+    def device_of(at_x, at_y):
+        return (at_x * SIDE + at_y) * CORES + core
+
     def along_group(offset):
         return (slab, (group + offset + GROUPS) % GROUPS)
 
@@ -114,7 +124,9 @@
         )
 
     load_grads = pltpu.make_async_copy(grads_hbm, grads_in, load_sem.at[0])
-    load_momentum = pltpu.make_async_copy(momentum_hbm, pair.at[0], load_sem.at[1])
+    load_momentum = pltpu.make_async_copy(momentum_hbm, pair.at[:, 0], load_sem.at[1])
+    load_slots = pltpu.make_async_copy(slot_hbm, slot_ref, load_sem.at[2])
+    load_slots.start()
     load_grads.start()
     load_momentum.start()
 
@@ -128,11 +140,12 @@
             barrier, inc=1, device_id=along_slab((slab + step) % SLABS), device_id_type=MESH
         )
 
+    load_slots.wait()
     load_grads.wait()
     total = jnp.zeros((8, K), jnp.float32)
     for expert in range(EXPERTS):
         block = grads_in[slot_ref[0, expert]]
-        pair[1, expert] = block
+        pair[expert, 1] = block
         total += squares(block)
     lanes = total[:, :128] + total[:, 128:256] + total[:, 256:384] + total[:, 384:]
     part[...] = jnp.sum(lanes, axis=0, keepdims=True)
@@ -152,43 +165,67 @@
     def _(step):
         slab_copy(step).start()
 
-    def raw_copies(hops, which):
+    def raw_route(hops, which):
         column = (x + hops) % SIDE
-        expert = column * 2 + which
         row = which * 2 + column % 2
-        place = ((x + SIDE - column) % SIDE) * SIDE + (y + SIDE - row) % SIDE
-        target = (column * SIDE + row) * CORES + core
-        index = COLUMNS.index(hops) * 2 + which
-        return target, expert, [
-            send(
-                pair.at[kind, expert],
-                raw.at[kind, place],
-                raw_send.at[kind, index],
-                raw_recv.at[kind, place],
-                along_slab(target),
-            )
-            for kind in range(2)
-        ]
-
-    def local_copies(expert):
-        return [
-            pltpu.make_async_copy(pair.at[kind, expert], raw.at[kind, 0], local_sem.at[kind])
-            for kind in range(2)
-        ]
-
-    for hops in COLUMNS:
-        for which in range(2):
-            target, expert, copies = raw_copies(hops, which)
-
-            @pl.when(target != slab)
-            def _():
-                for copy in copies:
-                    copy.start()
-
-    @pl.when(active)
-    def _():
-        for copy in local_copies(mine):
-            copy.start()
+        return (
+            column * 2 + which,
+            column,
+            row,
+            (SIDE - hops) % SIDE,
+            (y + SIDE - row) % SIDE,
+            COLUMNS.index(hops) * 2 + which,
+        )
+
+    def raw_direct(hops, which):
+        expert, column, row, from_x, from_y, index = raw_route(hops, which)
+        place = from_x * SIDE + from_y
+        return send(
+            pair.at[expert],
+            raw.at[place],
+            raw_send.at[index],
+            raw_recv.at[place],
+            along_slab(device_of(column, row)),
+        )
+
+    def raw_relayed(hops, which, slot, by_x, by_y):
+        expert, column, row, from_x, from_y, index = raw_route(hops, which)
+        return send(
+            pair.at[expert],
+            relayed.at[slot],
+            raw_send.at[index],
+            relay_recv.at[slot],
+            along_slab(device_of((column + by_x) % SIDE, (row + by_y) % SIDE)),
+        )
+
+    def relay_forward(slot):
+        if slot < 2:
+            towards = (x, (y + 1 + 2 * (y % 2)) % SIDE)
+            place = (1 + 2 * slot) * SIDE + 2
+        else:
+            towards = ((x + (3 if slot == 2 else 1)) % SIDE, y)
+            place = 5 if slot == 2 else 15
+        return send(
+            relayed.at[slot],
+            raw.at[place],
+            relay_send.at[slot],
+            raw_recv.at[place],
+            along_slab(device_of(*towards)),
+        )
+
+    def relay_wait(slot):
+        send(
+            pair.at[0], relayed.at[slot], raw_send.at[0], relay_recv.at[slot], along_slab(slab)
+        ).wait_recv()
+
+    def relay(slots):
+        @pl.when(jnp.logical_not(active))
+        def _():
+            for slot in slots:
+                relay_wait(slot)
+                relay_forward(slot).start()
+
+    local_copy = pltpu.make_async_copy(pair.at[mine], raw.at[0], local_sem.at[0])
 
     @pl.loop(1, SLABS)
     def _(step):
@@ -207,37 +244,69 @@
         for index, offset in enumerate(NEAR)
     ]
 
-    def step_copies(src, dst, stage):
+    def step_copies(src, dst, stage, reach):
         return [
             send(
-                src(side),
+                src,
                 dst.at[side],
                 step_send.at[stage, side],
                 step_recv.at[stage, side],
                 along_group(offset),
             )
-            for side, offset in enumerate((REACH, -REACH))
+            for side, offset in enumerate((reach, -reach))
         ]
 
-    window_copies = step_copies(lambda side: window, window_parts, 0)
-    wide_copies = step_copies(lambda side: wide_window, wide_parts, 1)
-    far_copies = step_copies(lambda side: wide_parts.at[side], far_parts, 2)
+    window_copies = step_copies(window, window_parts, 0, REACH)
+    far_copies = step_copies(wide_window, far_parts, 1, 2 * REACH)
 
     for copy in near_copies:
         copy.start()
+
+    for hops, diagonal in ((1, 3), (3, 1)):
+        for which in range(2):
+            from_y = raw_route(hops, which)[4]
+            row = raw_route(hops, which)[2]
+
+            @pl.when(from_y == diagonal)
+            def _():
+                raw_relayed(hops, which, 2 if diagonal == 1 else 3, SIDE - hops, 0).start()
+
+            @pl.when(from_y == 2)
+            def _():
+                raw_relayed(
+                    hops, which, 1 if diagonal == 3 else 0, 0, 1 + 2 * (row % 2)
+                ).start()
+
+    for hops in COLUMNS:
+        for which in range(2):
+            from_y = raw_route(hops, which)[4]
+            if hops == 0:
+                direct = from_y != 0
+            elif hops == 2:
+                direct = True
+            else:
+                direct = jnp.logical_and(from_y != 2, from_y != SIDE - hops)
+
+            @pl.when(direct)
+            def _():
+                raw_direct(hops, which).start()
+
+    @pl.when(active)
+    def _():
+        local_copy.start()
+
     for copy in near_copies:
         copy.wait_recv()
     window[...] = plane[...] + jnp.sum(near_parts[...], axis=0)
     for copy in window_copies:
         copy.start()
+    relay((2, 3))
     for copy in window_copies:
         copy.wait_recv()
     wide_window[...] = jnp.sum(window_parts[...], axis=0)
-    for copy in wide_copies:
+    for copy in far_copies:
         copy.start()
-    for copy, forward in zip(wide_copies, far_copies):
-        copy.wait_recv()
-        forward.start()
+    relay((0, 1))
     for copy in far_copies:
         copy.wait_recv()
 
@@ -247,7 +316,7 @@
 
     def own_result():
         for expert in range(EXPERTS):
-            new_ref[expert] = fresh(pair[0, expert], pair[1, expert], factor)
+            new_ref[expert] = fresh(pair[expert, 0], pair[expert, 1], factor)
 
     def gram_copies():
         partner = along_slab(chip * CORES + 1 - core)
@@ -264,7 +333,20 @@
 
     def back_copy(hops_x, hops_y):
         place = hops_x * SIDE + hops_y
-        target = ((x + hops_x) % SIDE * SIDE + (y + hops_y) % SIDE) * CORES + core
+        if (hops_x, hops_y) in BACK_RELAYED:
+            slot = BACK_RELAYED.index((hops_x, hops_y))
+            if slot < 2:
+                by = ((x + 3 + 2 * (x % 2)) % SIDE, y)
+            else:
+                by = (x, (y + hops_y) % SIDE)
+            return send(
+                outgoing.at[place],
+                back_relayed.at[slot],
+                back_send.at[place],
+                back_relay_recv.at[slot],
+                along_slab(device_of(*by)),
+            )
+        target = device_of((x + hops_x) % SIDE, (y + hops_y) % SIDE)
         return send(
             outgoing.at[place],
             update_ref.at[mine],
@@ -273,25 +355,43 @@
             along_slab(target),
         )
 
+    def back_forward(slot):
+        hops_x, hops_y = BACK_RELAYED[slot]
+        if slot < 2:
+            of_x, of_y = (x + 3 + 2 * (x % 2)) % SIDE, y
+        else:
+            of_x, of_y = x, (y + SIDE - hops_y) % SIDE
+        expert = of_x * 2 + of_y // 2
+        return send(
+            back_relayed.at[slot],
+            update_ref.at[expert],
+            back_relay_send.at[slot],
+            back_recv.at[expert],
+            along_slab(device_of((of_x + hops_x) % SIDE, (of_y + hops_y) % SIDE)),
+        )
+
+    def back_wait(slot):
+        send(
+            outgoing.at[0],
+            back_relayed.at[slot],
+            back_send.at[0],
+            back_relay_recv.at[slot],
+            along_slab(slab),
+        ).wait_recv()
+
     @pl.when(active)
     def _():
-        for copy in local_copies(mine):
-            copy.wait()
+        local_copy.wait()
 
         @pl.loop(1, CHIPS)
         def _(place):
-            for kind in range(2):
-                send(
-                    pair.at[kind, 0],
-                    raw.at[kind, place],
-                    raw_send.at[kind, 0],
-                    raw_recv.at[kind, place],
-                    along_slab(slab),
-                ).wait_recv()
+            send(
+                pair.at[0], raw.at[place], raw_send.at[0], raw_recv.at[place], along_slab(slab)
+            ).wait_recv()
 
         for place in range(CHIPS):
             own_new[place * ROWS : (place + 1) * ROWS, :] = fresh(
-                raw[0, place], raw[1, place], factor
+                raw[place, 0], raw[place, 1], factor
             )
 
         for index, (left, right) in enumerate(((0, 0), (0, 1), (1, 1))):
@@ -379,21 +479,32 @@
 
     own_result()
 
+    @pl.when(jnp.logical_not(active))
+    def _():
+        for slot in range(len(BACK_RELAYED)):
+            back_wait(slot)
+            back_forward(slot).start()
+
     for hops in COLUMNS:
         for which in range(2):
-            target, expert, copies = raw_copies(hops, which)
-
-            @pl.when(target != slab)
+            expert, column, row, from_x, from_y, index = raw_route(hops, which)
+
+            @pl.when(device_of(column, row) != slab)
             def _():
-                for copy in copies:
-                    copy.wait_send()
+                raw_direct(hops, which).wait_send()
                 send(
                     outgoing.at[0],
                     update_ref.at[expert],
                     back_send.at[0],
                     back_recv.at[expert],
-                    along_slab(target),
+                    along_slab(slab),
                 ).wait_recv()
+
+    @pl.when(jnp.logical_not(active))
+    def _():
+        for slot in range(len(BACK_RELAYED)):
+            relay_forward(slot).wait_send()
+            back_forward(slot).wait_send()
 
     @pl.when(active)
     def _():
@@ -408,7 +519,7 @@
     def _(step):
         slab_copy(step).wait_send()
 
-    for copy in near_copies + window_copies + wide_copies + far_copies:
+    for copy in near_copies + window_copies + far_copies:
         copy.wait_send()
 
 
@@ -420,15 +531,18 @@
         kernel,
         out_shape=(shape, shape),
         in_specs=[
-            pl.BlockSpec(memory_space=pltpu.SMEM),
-            pl.BlockSpec(memory_space=pl.ANY),
-            pl.BlockSpec(memory_space=pl.ANY),
+            pl.BlockSpec(memory_space=pltpu.HBM),
+            pl.BlockSpec(memory_space=pltpu.HBM),
+            pl.BlockSpec(memory_space=pltpu.HBM),
         ],
         out_specs=(pl.BlockSpec(memory_space=pltpu.VMEM),) * 2,
         scratch_shapes=[
+            pltpu.SMEM((1, EXPERTS), jnp.int32),
             pltpu.VMEM((EXPERTS, ROWS, K), jnp.bfloat16),
-            pltpu.VMEM((2, EXPERTS, ROWS, K), jnp.bfloat16),
-            pltpu.VMEM((2, CHIPS, ROWS, K), jnp.bfloat16),
+            pltpu.VMEM((EXPERTS, 2, ROWS, K), jnp.bfloat16),
+            pltpu.VMEM((CHIPS, 2, ROWS, K), jnp.bfloat16),
+            pltpu.VMEM((len(BACK_RELAYED), 2, ROWS, K), jnp.bfloat16),
+            pltpu.VMEM((len(BACK_RELAYED), ROWS, K), jnp.bfloat16),
             pltpu.VMEM((OWN, K), jnp.bfloat16),
             pltpu.VMEM(scalar, jnp.float32),
             pltpu.VMEM((SLABS, *scalar), jnp.float32),
@@ -437,7 +551,6 @@
             pltpu.VMEM(scalar, jnp.float32),
             pltpu.VMEM((2, *scalar), jnp.float32),
             pltpu.VMEM(scalar, jnp.float32),
-            pltpu.VMEM((2, *scalar), jnp.float32),
             pltpu.VMEM((2, *scalar), jnp.float32),
             pltpu.VMEM((3, HALF, HALF), jnp.float32),
             pltpu.VMEM((3, HALF, HALF), jnp.float32),
@@ -448,22 +561,28 @@
             pltpu.VMEM((K, K), jnp.bfloat16),
             pltpu.VMEM((K, K), jnp.bfloat16),
             pltpu.VMEM((CHIPS, ROWS, K), jnp.bfloat16),
-            dma((2,)),
+            dma((3,)),
             dma((SLABS,)),
             dma((SLABS,)),
             dma((len(NEAR),)),
             dma((len(NEAR),)),
-            dma((3, 2)),
-            dma((3, 2)),
-            dma((2, EXPERTS)),
-            dma((2, CHIPS)),
-            dma((2,)),
+            dma((2, 2)),
+            dma((2, 2)),
+            dma((EXPERTS,)),
+            dma((CHIPS,)),
+            dma((len(BACK_RELAYED),)),
+            dma((len(BACK_RELAYED),)),
+            dma((1,)),
             dma((3,)),
             dma((3,)),
             dma((CHIPS,)),
             dma((EXPERTS,)),
+            dma((len(BACK_RELAYED),)),
+            dma((len(BACK_RELAYED),)),
         ],
-        compiler_params=pltpu.CompilerParams(collective_id=0, has_side_effects=True),
+        compiler_params=pltpu.CompilerParams(
+            collective_id=0, has_side_effects=True, vmem_limit_bytes=48 * 1024 * 1024
+        ),
         name="muon_step",
     )(grad_slot, grads, momentum)
 

time: 87.9 us -> 69.3 us (0.79)
  Pallas kernels: 84.3 us -> 64.1 us
  local copies, waits for them, and re-layouts: 2.72 us -> 4.32 us
    pallas_call x1, Pallas kernels: 84.3 us -> 64.1 us  [on_device(): pl.pallas_call(kernel, out_shape=(shape, shape), in_specs=[pl.BlockSpec(m...]
    unnamed x4 -> x8, local copies, waits for them, and re-layouts: 2.72 us -> 4.32 us
where the time goes in v2:
time: 69.3 us; the launch traced here: 69.1 us
  Pallas kernels  64.1 us (92%)
  local copies, waits for them, and re-layouts  4.32 us (6%)
    pallas_call x1, Pallas kernels, on_device(): pl.pallas_call(kernel, out_shape=(shape, shape), in_specs=[pl.BlockSpec(m...  64.1 us
    unnamed x8, local copies, waits for them, and re-layouts  4.32 us

profile of v2, /device:TPU:1, one launch (start us, length us, event | category | flops | bytes accessed | tf_op | source)
XLA Modules:
  0.0 69.1 jit_solution(14760487645882321881)
XLA Ops:
  0.6 0.0 copy-start
  0.6 1.0 %copy-done = bf16[8,64,512]{2,1,0:T(8,128)(2,1)S(1)} copy-done((bf16[8,64,512]{2,1,0:T(8,128)(2,1)S(1)}, bf16[8,64,512]{2,1,0:T(8,128)(2,1)}, u32[]{:S(2)}) %copy-start) | copy-done | bytes 524312
  1.7 0.0 copy-start.1
  1.7 1.0 %copy-done.1 = bf16[8,64,512]{2,1,0:T(8,128)(2,1)S(1)} copy-done((bf16[8,64,512]{2,1,0:T(8,128)(2,1)S(1)}, bf16[8,64,512]{2,1,0:T(8,128)(2,1)}, u32[]{:S(2)}) %copy-start.1) | copy-done | bytes 524312
  2.7 0.0 copy-start.2
  2.7 0.7 copy-done.2
  3.4 64.1 %muon_step.1 = (bf16[8,64,512]{2,1,0:T(8,128)(2,1)S(1)}, bf16[8,64,512]{2,1,0:T(8,128)(2,1)S(1)}) custom-call(s32[1,8]{1,0:T(1,128)S(1)} %copy-done.2, bf16[8,64,512]{2,1,0:T(8,128)(2,1)S(1)} %copy-done, bf16[8,64,512]{2,1,0:T(8,128)(2,1)S(1)} %copy-done.1), custom_call_target="tpu_custom_call" | custom-call | tf_op jit(solution)/shard_map/muon_step/pallas_call | solution.py:530
  67.5 0.8 %copy.7 = bf16[8,64,512]{2,1,0:T(8,128)(2,1)} copy(bf16[8,64,512]{2,1,0:T(8,128)(2,1)S(1)} %get-tuple-element.4) | data formatting | bytes 1048576
  68.3 0.8 %copy.8 = bf16[8,64,512]{2,1,0:T(8,128)(2,1)} copy(bf16[8,64,512]{2,1,0:T(8,128)(2,1)S(1)} %get-tuple-element.5) | data formatting | bytes 1048576
Async XLA Ops:
  0.6 1.0 %copy-start = (bf16[8,64,512]{2,1,0:T(8,128)(2,1)S(1)}, bf16[8,64,512]{2,1,0:T(8,128)(2,1)}, u32[]{:S(2)}) copy-start(bf16[8,64,512]{2,1,0:T(8,128)(2,1)} %grads_hbm.1) | copy-start | bytes 1572868
  1.7 1.0 %copy-start.1 = (bf16[8,64,512]{2,1,0:T(8,128)(2,1)S(1)}, bf16[8,64,512]{2,1,0:T(8,128)(2,1)}, u32[]{:S(2)}) copy-start(bf16[8,64,512]{2,1,0:T(8,128)(2,1)} %momentum_hbm.1) | copy-start | bytes 1572868
  2.7 0.7 copy-start.2

commit v3 on v2

--- a/solution.py
+++ b/solution.py
@@ -58,6 +58,7 @@
     raw,
     relayed,
     back_relayed,
+    fresh_out,
     own_new,
     part,
     slab_parts,
@@ -300,13 +301,12 @@
     window[...] = plane[...] + jnp.sum(near_parts[...], axis=0)
     for copy in window_copies:
         copy.start()
-    relay((2, 3))
     for copy in window_copies:
         copy.wait_recv()
     wide_window[...] = jnp.sum(window_parts[...], axis=0)
     for copy in far_copies:
         copy.start()
-    relay((0, 1))
+    relay((2, 3, 0, 1))
     for copy in far_copies:
         copy.wait_recv()
 
@@ -316,7 +316,7 @@
 
     def own_result():
         for expert in range(EXPERTS):
-            new_ref[expert] = fresh(pair[expert, 0], pair[expert, 1], factor)
+            fresh_out[expert] = fresh(pair[expert, 0], pair[expert, 1], factor)
 
     def gram_copies():
         partner = along_slab(chip * CORES + 1 - core)
@@ -383,13 +383,11 @@
     def _():
         local_copy.wait()
 
-        @pl.loop(1, CHIPS)
-        def _(place):
-            send(
-                pair.at[0], raw.at[place], raw_send.at[0], raw_recv.at[place], along_slab(slab)
-            ).wait_recv()
-
         for place in range(CHIPS):
+            if place > 0:
+                send(
+                    pair.at[0], raw.at[place], raw_send.at[0], raw_recv.at[place], along_slab(slab)
+                ).wait_recv()
             own_new[place * ROWS : (place + 1) * ROWS, :] = fresh(
                 raw[place, 0], raw[place, 1], factor
             )
@@ -475,9 +473,11 @@
                     back_copy(COLUMNS[turn - 1], hops_y).start()
         for hops_y in COLUMNS[:-1]:
             back_copy(0, hops_y).start()
-        update_ref[mine] = outgoing[0]
+        pltpu.make_async_copy(outgoing.at[0], update_ref.at[mine], local_sem.at[1]).start()
 
     own_result()
+    new_copy = pltpu.make_async_copy(fresh_out, new_ref, load_sem.at[3])
+    new_copy.start()
 
     @pl.when(jnp.logical_not(active))
     def _():
@@ -506,8 +506,11 @@
             relay_forward(slot).wait_send()
             back_forward(slot).wait_send()
 
+    new_copy.wait()
+
     @pl.when(active)
     def _():
+        pltpu.make_async_copy(outgoing.at[0], update_ref.at[mine], local_sem.at[1]).wait()
         for copy in gram_copies():
             copy.wait_send()
         for hops_x in COLUMNS:
@@ -523,11 +526,38 @@
         copy.wait_send()
 
 
+def finish_kernel(new_ref, update_ref, new_out, update_out, sem):
+    copies = (
+        pltpu.make_async_copy(new_ref, new_out, sem.at[0]),
+        pltpu.make_async_copy(update_ref, update_out, sem.at[1]),
+    )
+    for copy in copies:
+        copy.start()
+    for copy in copies:
+        copy.wait()
+
+
+def finish(new, update):
+    anywhere = (pl.BlockSpec(memory_space=pl.ANY),) * 2
+    return pl.pallas_call(
+        finish_kernel,
+        out_shape=tuple(jax.ShapeDtypeStruct(a.shape, a.dtype) for a in (new, update)),
+        in_specs=anywhere,
+        out_specs=anywhere,
+        scratch_shapes=[pltpu.SemaphoreType.DMA((2,))],
+        compiler_params=pltpu.CompilerParams(vmem_limit_bytes=1024 * 1024),
+        name="finish",
+    )(new, update)
+
+
 def on_device(grads, grad_slot, momentum):
-    shape = jax.ShapeDtypeStruct(grads.shape, jnp.bfloat16)
+    shape = pltpu.VMEM(grads.shape, jnp.bfloat16)
+    grads, grad_slot, momentum = (
+        pltpu.with_memory_space_constraint(a, pltpu.HBM) for a in (grads, grad_slot, momentum)
+    )
     scalar = (1, 128)
     dma = pltpu.SemaphoreType.DMA
-    return pl.pallas_call(
+    return finish(*pl.pallas_call(
         kernel,
         out_shape=(shape, shape),
         in_specs=[
@@ -535,7 +565,7 @@
             pl.BlockSpec(memory_space=pltpu.HBM),
             pl.BlockSpec(memory_space=pltpu.HBM),
         ],
-        out_specs=(pl.BlockSpec(memory_space=pltpu.VMEM),) * 2,
+        out_specs=(pl.BlockSpec(memory_space=pl.ANY),) * 2,
         scratch_shapes=[
             pltpu.SMEM((1, EXPERTS), jnp.int32),
             pltpu.VMEM((EXPERTS, ROWS, K), jnp.bfloat16),
@@ -543,6 +573,7 @@
             pltpu.VMEM((CHIPS, 2, ROWS, K), jnp.bfloat16),
             pltpu.VMEM((len(BACK_RELAYED), 2, ROWS, K), jnp.bfloat16),
             pltpu.VMEM((len(BACK_RELAYED), ROWS, K), jnp.bfloat16),
+            pltpu.VMEM((EXPERTS, ROWS, K), jnp.bfloat16),
             pltpu.VMEM((OWN, K), jnp.bfloat16),
             pltpu.VMEM(scalar, jnp.float32),
             pltpu.VMEM((SLABS, *scalar), jnp.float32),
@@ -561,7 +592,7 @@
             pltpu.VMEM((K, K), jnp.bfloat16),
             pltpu.VMEM((K, K), jnp.bfloat16),
             pltpu.VMEM((CHIPS, ROWS, K), jnp.bfloat16),
-            dma((3,)),
+            dma((4,)),
             dma((SLABS,)),
             dma((SLABS,)),
             dma((len(NEAR),)),
@@ -572,7 +603,7 @@
             dma((CHIPS,)),
             dma((len(BACK_RELAYED),)),
             dma((len(BACK_RELAYED),)),
-            dma((1,)),
+            dma((2,)),
             dma((3,)),
             dma((3,)),
             dma((CHIPS,)),
@@ -584,7 +615,7 @@
             collective_id=0, has_side_effects=True, vmem_limit_bytes=48 * 1024 * 1024
         ),
         name="muon_step",
-    )(grad_slot, grads, momentum)
+    )(grad_slot, grads, momentum))
 
 
 def solution(mesh):

time: 69.3 us -> 65.9 us (0.951)
  local copies, waits for them, and re-layouts: 4.32 us -> 0 us
  Pallas kernels: 64.1 us -> 65.1 us
    unnamed x8 -> x0, local copies, waits for them, and re-layouts: 4.32 us -> none
    pallas_call x0 -> x1, Pallas kernels: none -> 0.99 us  [finish(): pl.pallas_call(finish_kernel, out_shape=tuple((jax.ShapeDtypeStruct(a.sha...]
where the time goes in v3:
time: 65.9 us; the launch traced here: 65.7 us
  Pallas kernels  65.1 us (99%)
    pallas_call x1, Pallas kernels, on_device(): pl.pallas_call(kernel, out_shape=(shape, shape), in_specs=[pl.BlockSpec(m...  64.1 us

profile of v3, /device:TPU:1, one launch (start us, length us, event | category | flops | bytes accessed | tf_op | source)
XLA Modules:
  0.0 65.7 jit_solution(5180146644850963636)
XLA Ops:
  0.6 64.1 %muon_step.1 = (bf16[8,64,512]{2,1,0:T(8,128)(2,1)S(1)}, bf16[8,64,512]{2,1,0:T(8,128)(2,1)S(1)}) custom-call(s32[1,8]{1,0:T(1,128)} %slot_hbm.1, bf16[8,64,512]{2,1,0:T(8,128)(2,1)} %grads_hbm.1, bf16[8,64,512]{2,1,0:T(8,128)(2,1)} %momentum_hbm.1), custom_call_target="tpu_custom_call" | custom-call | tf_op jit(solution)/shard_map/muon_step/pallas_call | solution.py:560
  64.7 1.0 %finish.1 = (bf16[8,64,512]{2,1,0:T(8,128)(2,1)}, bf16[8,64,512]{2,1,0:T(8,128)(2,1)}) custom-call(bf16[8,64,512]{2,1,0:T(8,128)(2,1)S(1)} %get-tuple-element.4.new_ref, bf16[8,64,512]{2,1,0:T(8,128)(2,1)S(1)} %get-tuple-element.5.update_ref), custom_call_target="tpu_custom_call" | custom-call | tf_op jit(solution)/shard_map/finish/pallas_call | solution.py:542

commit v4 on v3

--- a/solution.py
+++ b/solution.py
@@ -28,7 +28,8 @@
 
 COLUMNS = (2, 1, 3, 0)
 BACK_RELAYED = ((2, 1), (2, 3), (1, 1), (3, 3))
-NEAR = tuple(off for off in range(-REACH, REACH) if off != 0)
+GREETED = tuple(off for off in range(-REACH, REACH + 1) if off != 0)
+NEAR = tuple(sorted((off for off in range(-2 * REACH, 2 * REACH) if off != 0), key=lambda o: -abs(o)))
 
 
 def squares(block):
@@ -65,9 +66,8 @@
     plane,
     near_parts,
     window,
-    window_parts,
-    wide_window,
     far_parts,
+    grand,
     gram_own,
     gram_other,
     current,
@@ -82,8 +82,12 @@
     slab_recv,
     near_send,
     near_recv,
-    step_send,
-    step_recv,
+    far_send,
+    far_recv,
+    grand_send,
+    grand_recv,
+    greeting,
+    passed,
     raw_send,
     raw_recv,
     relay_send,
@@ -131,9 +135,19 @@
     load_grads.start()
     load_momentum.start()
 
+    along = core == 1
+    unseen = jnp.maximum(REACH - group, 0)
     barrier = pltpu.get_barrier_semaphore()
-    for offset in NEAR + (REACH,):
-        pl.semaphore_signal(barrier, inc=1, device_id=along_group(offset), device_id_type=MESH)
+
+    @pl.when(along)
+    def _():
+        for offset in GREETED:
+
+            @pl.when(group + offset < GROUPS)
+            def _():
+                pl.semaphore_signal(
+                    barrier, inc=1, device_id=along_group(offset), device_id_type=MESH
+                )
 
     @pl.loop(1, SLABS)
     def _(step):
@@ -151,7 +165,7 @@
     lanes = total[:, :128] + total[:, 128:256] + total[:, 256:384] + total[:, 384:]
     part[...] = jnp.sum(lanes, axis=0, keepdims=True)
     load_momentum.wait()
-    pl.semaphore_wait(barrier, SLABS - 1 + len(NEAR) + 1)
+    pl.semaphore_wait(barrier, SLABS - 1 + core * (len(GREETED) - unseen))
 
     def slab_copy(step):
         return send(
@@ -165,6 +179,26 @@
     @pl.loop(1, SLABS)
     def _(step):
         slab_copy(step).start()
+
+    def pass_on():
+        for side, offset in enumerate((REACH, -REACH)):
+            pl.semaphore_signal(
+                passed.at[side], inc=1, device_id=along_group(offset), device_id_type=MESH
+            )
+
+    @pl.when(along)
+    def _():
+        for offset in range(1, REACH + 1):
+
+            @pl.when(group + offset >= GROUPS)
+            def _():
+                pl.semaphore_signal(
+                    greeting, inc=1, device_id=along_group(offset), device_id_type=MESH
+                )
+
+        @pl.when(unseen == 0)
+        def _():
+            pass_on()
 
     def raw_route(hops, which):
         column = (x + hops) % SIDE
@@ -245,23 +279,29 @@
         for index, offset in enumerate(NEAR)
     ]
 
-    def step_copies(src, dst, stage, reach):
-        return [
-            send(
-                src,
-                dst.at[side],
-                step_send.at[stage, side],
-                step_recv.at[stage, side],
-                along_group(offset),
-            )
-            for side, offset in enumerate((reach, -reach))
-        ]
-
-    window_copies = step_copies(window, window_parts, 0, REACH)
-    far_copies = step_copies(wide_window, far_parts, 1, 2 * REACH)
-
-    for copy in near_copies:
-        copy.start()
+    far_copies = [
+        send(
+            window,
+            far_parts.at[side],
+            far_send.at[side],
+            far_recv.at[side],
+            along_group(offset),
+        )
+        for side, offset in enumerate((2 * REACH, -2 * REACH))
+    ]
+    grand_copy = send(
+        grand, grand, grand_send.at[0], grand_recv.at[0], along_slab(chip * CORES + 1 - core)
+    )
+
+    def start_near():
+        for side in range(2):
+            pl.semaphore_wait(passed.at[side], 1)
+        for copy in near_copies:
+            copy.start()
+
+    @pl.when(jnp.logical_and(along, unseen == 0))
+    def _():
+        start_near()
 
     for hops, diagonal in ((1, 3), (3, 1)):
         for which in range(2):
@@ -296,21 +336,31 @@
     def _():
         local_copy.start()
 
-    for copy in near_copies:
-        copy.wait_recv()
-    window[...] = plane[...] + jnp.sum(near_parts[...], axis=0)
-    for copy in window_copies:
-        copy.start()
-    for copy in window_copies:
-        copy.wait_recv()
-    wide_window[...] = jnp.sum(window_parts[...], axis=0)
-    for copy in far_copies:
-        copy.start()
-    relay((2, 3, 0, 1))
-    for copy in far_copies:
-        copy.wait_recv()
-
-    total_sq = jnp.sum(jnp.sum(far_parts[...], axis=0), axis=1, keepdims=True)
+    @pl.when(jnp.logical_and(along, unseen > 0))
+    def _():
+        pl.semaphore_wait(greeting, unseen)
+        pass_on()
+        start_near()
+
+    @pl.when(along)
+    def _():
+        for copy in near_copies:
+            copy.wait_recv()
+        window[...] = plane[...] + jnp.sum(near_parts[...], axis=0)
+        for copy in far_copies:
+            copy.start()
+        relay((2, 3, 0, 1))
+        for copy in far_copies:
+            copy.wait_recv()
+        grand[...] = jnp.sum(far_parts[...], axis=0)
+        grand_copy.start()
+
+    @pl.when(jnp.logical_not(along))
+    def _():
+        relay((2, 3, 0, 1))
+        grand_copy.wait_recv()
+
+    total_sq = jnp.sum(grand[...], axis=1, keepdims=True)
     root_mean = jnp.sqrt(total_sq / ENTRIES + 1e-06)
     factor = jnp.minimum(1.0, 1.0 / root_mean)
 
@@ -522,8 +572,10 @@
     def _(step):
         slab_copy(step).wait_send()
 
-    for copy in near_copies + window_copies + far_copies:
-        copy.wait_send()
+    @pl.when(along)
+    def _():
+        for copy in near_copies + far_copies + [grand_copy]:
+            copy.wait_send()
 
 
 def finish_kernel(new_ref, update_ref, new_out, update_out, sem):
@@ -582,7 +634,6 @@
             pltpu.VMEM(scalar, jnp.float32),
             pltpu.VMEM((2, *scalar), jnp.float32),
             pltpu.VMEM(scalar, jnp.float32),
-            pltpu.VMEM((2, *scalar), jnp.float32),
             pltpu.VMEM((3, HALF, HALF), jnp.float32),
             pltpu.VMEM((3, HALF, HALF), jnp.float32),
             pltpu.VMEM((K, K), jnp.float32),
@@ -597,8 +648,12 @@
             dma((SLABS,)),
             dma((len(NEAR),)),
             dma((len(NEAR),)),
-            dma((2, 2)),
-            dma((2, 2)),
+            dma((2,)),
+            dma((2,)),
+            dma((1,)),
+            dma((1,)),
+            pltpu.SemaphoreType.REGULAR,
+            pltpu.SemaphoreType.REGULAR((2,)),
             dma((EXPERTS,)),
             dma((CHIPS,)),
             dma((len(BACK_RELAYED),)),

time: 65.9 us -> 59.8 us (0.907)
  Pallas kernels: 65.1 us -> 59 us
    pallas_call x1, Pallas kernels: 64.1 us -> 58 us  [on_device(): pl.pallas_call(kernel, out_shape=(shape, shape), in_specs=[pl.BlockSpec(m...]
where the time goes in v4:
time: 59.8 us; the launch traced here: 59.6 us
  Pallas kernels  59 us (99%)
  between operations  0.64 us (1%)
    pallas_call x1, Pallas kernels, on_device(): pl.pallas_call(kernel, out_shape=(shape, shape), in_specs=[pl.BlockSpec(m...  58 us

profile of v4, /device:TPU:1, one launch (start us, length us, event | category | flops | bytes accessed | tf_op | source)
XLA Modules:
  0.0 59.6 jit_solution(3378671977371616131)
XLA Ops:
  0.6 58.0 %muon_step.1 = (bf16[8,64,512]{2,1,0:T(8,128)(2,1)S(1)}, bf16[8,64,512]{2,1,0:T(8,128)(2,1)S(1)}) custom-call(s32[1,8]{1,0:T(1,128)} %slot_hbm.1, bf16[8,64,512]{2,1,0:T(8,128)(2,1)} %grads_hbm.1, bf16[8,64,512]{2,1,0:T(8,128)(2,1)} %momentum_hbm.1), custom_call_target="tpu_custom_call" | custom-call | tf_op jit(solution)/shard_map/muon_step/pallas_call | solution.py:612
  58.6 1.0 %finish.1 = (bf16[8,64,512]{2,1,0:T(8,128)(2,1)}, bf16[8,64,512]{2,1,0:T(8,128)(2,1)}) custom-call(bf16[8,64,512]{2,1,0:T(8,128)(2,1)S(1)} %get-tuple-element.4.new_ref, bf16[8,64,512]{2,1,0:T(8,128)(2,1)S(1)} %get-tuple-element.5.update_ref), custom_call_target="tpu_custom_call" | custom-call | tf_op jit(solution)/shard_map/finish/pallas_call | solution.py:594

commit v5 on v4

--- a/solution.py
+++ b/solution.py
@@ -28,6 +28,19 @@
 
 COLUMNS = (2, 1, 3, 0)
 BACK_RELAYED = ((2, 1), (2, 3), (1, 1), (3, 3))
+ORDER = tuple((hops_x, hops_y) for hops_x in COLUMNS for hops_y in COLUMNS)
+AROUND = tuple(
+    sorted(
+        (
+            (hops_x, hops_y, other)
+            for hops_x in range(SIDE)
+            for hops_y in range(SIDE)
+            for other in range(CORES)
+            if (hops_x, hops_y, other) != (0, 0, 0)
+        ),
+        key=lambda h: -min(h[0], SIDE - h[0]) - min(h[1], SIDE - h[1]),
+    )
+)
 GREETED = tuple(off for off in range(-REACH, REACH + 1) if off != 0)
 NEAR = tuple(sorted((off for off in range(-2 * REACH, 2 * REACH) if off != 0), key=lambda o: -abs(o)))
 
@@ -67,7 +80,6 @@
     near_parts,
     window,
     far_parts,
-    grand,
     gram_own,
     gram_other,
     current,
@@ -84,8 +96,6 @@
     near_recv,
     far_send,
     far_recv,
-    grand_send,
-    grand_recv,
     greeting,
     passed,
     raw_send,
@@ -115,6 +125,10 @@
     def device_of(at_x, at_y):
         return (at_x * SIDE + at_y) * CORES + core
 
+    def around(hops):
+        hops_x, hops_y, other = hops
+        return ((x + hops_x) % SIDE * SIDE + (y + hops_y) % SIDE) * CORES + (core + other) % CORES
+
     def along_group(offset):
         return (slab, (group + offset + GROUPS) % GROUPS)
 
@@ -149,10 +163,9 @@
                     barrier, inc=1, device_id=along_group(offset), device_id_type=MESH
                 )
 
-    @pl.loop(1, SLABS)
-    def _(step):
+    for hops in AROUND:
         pl.semaphore_signal(
-            barrier, inc=1, device_id=along_slab((slab + step) % SLABS), device_id_type=MESH
+            barrier, inc=1, device_id=along_slab(around(hops)), device_id_type=MESH
         )
 
     load_slots.wait()
@@ -167,18 +180,18 @@
     load_momentum.wait()
     pl.semaphore_wait(barrier, SLABS - 1 + core * (len(GREETED) - unseen))
 
-    def slab_copy(step):
-        return send(
+    slab_copies = [
+        send(
             part,
-            slab_parts.at[step],
-            slab_send.at[step],
-            slab_recv.at[step],
-            along_slab((slab + step) % SLABS),
-        )
-
-    @pl.loop(1, SLABS)
-    def _(step):
-        slab_copy(step).start()
+            slab_parts.at[index],
+            slab_send.at[index],
+            slab_recv.at[index],
+            along_slab(around(hops)),
+        )
+        for index, hops in enumerate(AROUND)
+    ]
+    for copy in slab_copies:
+        copy.start()
 
     def pass_on():
         for side, offset in enumerate((REACH, -REACH)):
@@ -262,11 +275,10 @@
 
     local_copy = pltpu.make_async_copy(pair.at[mine], raw.at[0], local_sem.at[0])
 
-    @pl.loop(1, SLABS)
-    def _(step):
-        slab_copy(step).wait_recv()
-
-    plane[...] = part[...] + jnp.sum(slab_parts[1:], axis=0)
+    for copy in slab_copies:
+        copy.wait_recv()
+
+    plane[...] = part[...] + jnp.sum(slab_parts[...], axis=0)
 
     near_copies = [
         send(
@@ -283,15 +295,13 @@
         send(
             window,
             far_parts.at[side],
-            far_send.at[side],
+            far_send.at[receiver, side],
             far_recv.at[side],
-            along_group(offset),
-        )
+            (chip * CORES + receiver, (group + offset + GROUPS) % GROUPS),
+        )
+        for receiver in range(CORES)
         for side, offset in enumerate((2 * REACH, -2 * REACH))
     ]
-    grand_copy = send(
-        grand, grand, grand_send.at[0], grand_recv.at[0], along_slab(chip * CORES + 1 - core)
-    )
 
     def start_near():
         for side in range(2):
@@ -350,17 +360,15 @@
         for copy in far_copies:
             copy.start()
         relay((2, 3, 0, 1))
-        for copy in far_copies:
-            copy.wait_recv()
-        grand[...] = jnp.sum(far_parts[...], axis=0)
-        grand_copy.start()
 
     @pl.when(jnp.logical_not(along))
     def _():
         relay((2, 3, 0, 1))
-        grand_copy.wait_recv()
-
-    total_sq = jnp.sum(grand[...], axis=1, keepdims=True)
+
+    for copy in far_copies[:2]:
+        copy.wait_recv()
+
+    total_sq = jnp.sum(jnp.sum(far_parts[...], axis=0), axis=1, keepdims=True)
     root_mean = jnp.sqrt(total_sq / ENTRIES + 1e-06)
     factor = jnp.minimum(1.0, 1.0 / root_mean)
 
@@ -381,8 +389,9 @@
             for index in range(3)
         ]
 
-    def back_copy(hops_x, hops_y):
-        place = hops_x * SIDE + hops_y
+    def back_copy(hops):
+        hops_x, hops_y = hops
+        place = ORDER.index(hops)
         if (hops_x, hops_y) in BACK_RELAYED:
             slot = BACK_RELAYED.index((hops_x, hops_y))
             if slot < 2:
@@ -438,7 +447,8 @@
                 send(
                     pair.at[0], raw.at[place], raw_send.at[0], raw_recv.at[place], along_slab(slab)
                 ).wait_recv()
-            own_new[place * ROWS : (place + 1) * ROWS, :] = fresh(
+            row = ORDER.index((place // SIDE, place % SIDE)) * ROWS
+            own_new[row : row + ROWS, :] = fresh(
                 raw[place, 0], raw[place, 1], factor
             )
 
@@ -510,20 +520,20 @@
                 jnp.bfloat16
             )
 
-        for turn, hops_x in enumerate(COLUMNS):
-            start = hops_x * SIDE * ROWS
+        for turn in range(SIDE):
+            start = turn * SIDE * ROWS
             result = jnp.sqrt(jnp.float32(M)) * dot(
                 own_new[start : start + SIDE * ROWS, :], scaled[...]
             )
-            outgoing[hops_x * SIDE : (hops_x + 1) * SIDE] = result.astype(jnp.bfloat16).reshape(
+            outgoing[turn * SIDE : (turn + 1) * SIDE] = result.astype(jnp.bfloat16).reshape(
                 SIDE, ROWS, K
             )
             if turn > 0:
-                for hops_y in COLUMNS:
-                    back_copy(COLUMNS[turn - 1], hops_y).start()
-        for hops_y in COLUMNS[:-1]:
-            back_copy(0, hops_y).start()
-        pltpu.make_async_copy(outgoing.at[0], update_ref.at[mine], local_sem.at[1]).start()
+                for hops in ORDER[(turn - 1) * SIDE : turn * SIDE]:
+                    back_copy(hops).start()
+        for hops in ORDER[(SIDE - 1) * SIDE : -1]:
+            back_copy(hops).start()
+        pltpu.make_async_copy(outgoing.at[CHIPS - 1], update_ref.at[mine], local_sem.at[1]).start()
 
     own_result()
     new_copy = pltpu.make_async_copy(fresh_out, new_ref, load_sem.at[3])
@@ -560,29 +570,27 @@
 
     @pl.when(active)
     def _():
-        pltpu.make_async_copy(outgoing.at[0], update_ref.at[mine], local_sem.at[1]).wait()
+        pltpu.make_async_copy(outgoing.at[CHIPS - 1], update_ref.at[mine], local_sem.at[1]).wait()
         for copy in gram_copies():
             copy.wait_send()
-        for hops_x in COLUMNS:
-            for hops_y in COLUMNS:
-                if (hops_x, hops_y) != (0, 0):
-                    back_copy(hops_x, hops_y).wait_send()
-
-    @pl.loop(1, SLABS)
-    def _(step):
-        slab_copy(step).wait_send()
+        for hops in ORDER[:-1]:
+            back_copy(hops).wait_send()
+
+    for copy in slab_copies:
+        copy.wait_send()
 
     @pl.when(along)
     def _():
-        for copy in near_copies + far_copies + [grand_copy]:
+        for copy in near_copies + far_copies:
             copy.wait_send()
 
 
 def finish_kernel(new_ref, update_ref, new_out, update_out, sem):
-    copies = (
-        pltpu.make_async_copy(new_ref, new_out, sem.at[0]),
-        pltpu.make_async_copy(update_ref, update_out, sem.at[1]),
-    )
+    copies = [
+        pltpu.make_async_copy(src.at[expert], dst.at[expert], sem.at[which, expert])
+        for which, (src, dst) in enumerate(((new_ref, new_out), (update_ref, update_out)))
+        for expert in range(EXPERTS)
+    ]
     for copy in copies:
         copy.start()
     for copy in copies:
@@ -596,7 +604,7 @@
         out_shape=tuple(jax.ShapeDtypeStruct(a.shape, a.dtype) for a in (new, update)),
         in_specs=anywhere,
         out_specs=anywhere,
-        scratch_shapes=[pltpu.SemaphoreType.DMA((2,))],
+        scratch_shapes=[pltpu.SemaphoreType.DMA((2, EXPERTS))],
         compiler_params=pltpu.CompilerParams(vmem_limit_bytes=1024 * 1024),
         name="finish",
     )(new, update)
@@ -628,12 +636,11 @@
             pltpu.VMEM((EXPERTS, ROWS, K), jnp.bfloat16),
             pltpu.VMEM((OWN, K), jnp.bfloat16),
             pltpu.VMEM(scalar, jnp.float32),
-            pltpu.VMEM((SLABS, *scalar), jnp.float32),
+            pltpu.VMEM((SLABS - 1, *scalar), jnp.float32),
             pltpu.VMEM(scalar, jnp.float32),
             pltpu.VMEM((len(NEAR), *scalar), jnp.float32),
             pltpu.VMEM(scalar, jnp.float32),
             pltpu.VMEM((2, *scalar), jnp.float32),
-            pltpu.VMEM(scalar, jnp.float32),
             pltpu.VMEM((3, HALF, HALF), jnp.float32),
             pltpu.VMEM((3, HALF, HALF), jnp.float32),
             pltpu.VMEM((K, K), jnp.float32),
@@ -648,10 +655,8 @@
             dma((SLABS,)),
             dma((len(NEAR),)),
             dma((len(NEAR),)),
+            dma((2, 2)),
             dma((2,)),
-            dma((2,)),
-            dma((1,)),
-            dma((1,)),
             pltpu.SemaphoreType.REGULAR,
             pltpu.SemaphoreType.REGULAR((2,)),
             dma((EXPERTS,)),

time: 59.8 us -> 59.1 us (0.988)
  Pallas kernels: 59 us -> 57.9 us
    pallas_call x1, Pallas kernels: 58 us -> 56.8 us  [on_device(): pl.pallas_call(kernel, out_shape=(shape, shape), in_specs=[pl.BlockSpec(m...]
where the time goes in v5:
time: 59.1 us; the launch traced here: 58.6 us
  Pallas kernels  57.9 us (98%)
  between operations  0.64 us (1%)
    pallas_call x1, Pallas kernels, on_device(): pl.pallas_call(kernel, out_shape=(shape, shape), in_specs=[pl.BlockSpec(m...  56.8 us

profile of v5, /device:TPU:1, one launch (start us, length us, event | category | flops | bytes accessed | tf_op | source)
XLA Modules:
  0.0 58.6 jit_solution(17327899074926478445)
XLA Ops:
  0.6 56.8 %muon_step.1 = (bf16[8,64,512]{2,1,0:T(8,128)(2,1)S(1)}, bf16[8,64,512]{2,1,0:T(8,128)(2,1)S(1)}) custom-call(s32[1,8]{1,0:T(1,128)} %slot_hbm.1, bf16[8,64,512]{2,1,0:T(8,128)(2,1)} %grads_hbm.1, bf16[8,64,512]{2,1,0:T(8,128)(2,1)} %momentum_hbm.1), custom_call_target="tpu_custom_call" | custom-call | tf_op jit(solution)/shard_map/muon_step/pallas_call | solution.py:620
  57.5 1.1 %finish.1 = (bf16[8,64,512]{2,1,0:T(8,128)(2,1)}, bf16[8,64,512]{2,1,0:T(8,128)(2,1)}) custom-call(bf16[8,64,512]{2,1,0:T(8,128)(2,1)S(1)} %get-tuple-element.4.new_ref, bf16[8,64,512]{2,1,0:T(8,128)(2,1)S(1)} %get-tuple-element.5.update_ref), custom_call_target="tpu_custom_call" | custom-call | tf_op jit(solution)/shard_map/finish/pallas_call | solution.py:602

commit v6 on v5

--- a/solution.py
+++ b/solution.py
@@ -41,6 +41,7 @@
         key=lambda h: -min(h[0], SIDE - h[0]) - min(h[1], SIDE - h[1]),
     )
 )
+BLOCKS = ((0, 0), (1, 1), (0, 1))
 GREETED = tuple(off for off in range(-REACH, REACH + 1) if off != 0)
 NEAR = tuple(sorted((off for off in range(-2 * REACH, 2 * REACH) if off != 0), key=lambda o: -abs(o)))
 
@@ -452,21 +453,19 @@
                 raw[place, 0], raw[place, 1], factor
             )
 
-        for index, (left, right) in enumerate(((0, 0), (0, 1), (1, 1))):
+        for index, (left, right) in enumerate(BLOCKS):
             gram_own[index] = lax.dot_general(
                 own_new[:, left * HALF : (left + 1) * HALF],
                 own_new[:, right * HALF : (right + 1) * HALF],
                 (((0,), (0,)), ((), ())),
                 preferred_element_type=jnp.float32,
             )
-            if index > 0:
-                gram_copies()[index - 1].start()
-        gram_copies()[2].start()
-        for copy in gram_copies():
+            gram_copies()[index].start()
+        for copy in gram_copies()[:2]:
             copy.wait_recv()
 
         trace = jnp.zeros((128, 128), jnp.float32)
-        for index in (0, 2):
+        for index in range(2):
             whole = gram_own[index] + gram_other[index]
             gram_own_low, gram_own_high = whole[:128, :128], whole[128:, 128:]
             trace += gram_own_low + gram_own_high
@@ -478,13 +477,15 @@
             jnp.sum(jnp.sum(trace, axis=0, keepdims=True), axis=1, keepdims=True) + 1e-06
         )
         inverse = 1.0 / frobenius
-        for index, (left, right) in enumerate(((0, 0), (0, 1), (1, 1))):
+        for index, (left, right) in enumerate(BLOCKS):
+            if index == 2:
+                gram_copies()[2].wait_recv()
             block = (gram_own[index] + gram_other[index]) * inverse
             current[left * HALF : (left + 1) * HALF, right * HALF : (right + 1) * HALF] = block
             rounded[left * HALF : (left + 1) * HALF, right * HALF : (right + 1) * HALF] = (
                 block.astype(jnp.bfloat16)
             )
-            if index == 1:
+            if index == 2:
                 block = block.T
                 current[HALF:, :HALF] = block
                 rounded[HALF:, :HALF] = block.astype(jnp.bfloat16)

time: 59.1 us -> 58.9 us (level)
  no operation moved by 1% of the time
where the time goes in v6:
time: 58.9 us; the launch traced here: 58.3 us
  Pallas kernels  57.7 us (98%)
  between operations  0.64 us (1%)
    pallas_call x1, Pallas kernels, on_device(): pl.pallas_call(kernel, out_shape=(shape, shape), in_specs=[pl.BlockSpec(m...  56.6 us

profile of v6, /device:TPU:1, one launch (start us, length us, event | category | flops | bytes accessed | tf_op | source)
XLA Modules:
  0.0 58.3 jit_solution(14496969903843898162)
XLA Ops:
  0.6 56.6 %muon_step.1 = (bf16[8,64,512]{2,1,0:T(8,128)(2,1)S(1)}, bf16[8,64,512]{2,1,0:T(8,128)(2,1)S(1)}) custom-call(s32[1,8]{1,0:T(1,128)} %slot_hbm.1, bf16[8,64,512]{2,1,0:T(8,128)(2,1)} %grads_hbm.1, bf16[8,64,512]{2,1,0:T(8,128)(2,1)} %momentum_hbm.1), custom_call_target="tpu_custom_call" | custom-call | tf_op jit(solution)/shard_map/muon_step/pallas_call | solution.py:621
  57.2 1.1 %finish.1 = (bf16[8,64,512]{2,1,0:T(8,128)(2,1)}, bf16[8,64,512]{2,1,0:T(8,128)(2,1)}) custom-call(bf16[8,64,512]{2,1,0:T(8,128)(2,1)S(1)} %get-tuple-element.4.new_ref, bf16[8,64,512]{2,1,0:T(8,128)(2,1)S(1)} %get-tuple-element.5.update_ref), custom_call_target="tpu_custom_call" | custom-call | tf_op jit(solution)/shard_map/finish/pallas_call | solution.py:603
